TPU v7x, 32 devices: a whole 2x2x4 slice. The times are simulated.
32 devices in a mesh: dp: 2 (over x), ha: 4 (over z), wa: 4 (over y, core).
Axes of the slice: x: 2, y: 2, z: 4, core: 2. Of those that a mesh axis runs over, the one named last changes fastest.
Arguments:
- query_in: bfloat16 [2, 4, 4, 384, 512], P('dp', 'ha', 'wa'), may hold values from -30 to 30
- key_in: bfloat16 [2, 4, 4, 384, 512], P('dp', 'ha', 'wa'), may hold values from -6 to 6
- value_in: bfloat16 [2, 4, 4, 384, 512], P('dp', 'ha', 'wa'), may hold values from -6 to 6
- grad_out: bfloat16 [2, 4, 4, 384, 3072], P('dp', 'ha', 'wa'), may hold values from -1.5 to 1.5
- out_weight: bfloat16 [512, 3072], P('dp'), may hold values from -0.25 to 0.25
Outputs:
- outcome: bfloat16 [2, 4, 4, 384, 3072], P('dp', 'ha', 'wa')
- query_grad: float32 [2, 4, 4, 384, 512], P('dp', 'ha', 'wa')
- key_grad: float32 [2, 4, 4, 384, 512], P('dp', 'ha', 'wa')
- value_grad: float32 [2, 4, 4, 384, 512], P('dp', 'ha', 'wa')
- weight_grad: float32 [512, 3072], P('dp')
All inputs are finite; a program needn't handle non-finite values.
Results may differ from a plain program's by a relative error of at most 0.035.
Values may be sent and summed in bfloat16 or wider, within the bound.
No kernel may reach another device: no remote copies, remote signals or barrier semaphores. Data moves between devices by JAX's collectives and lax.ppermute only.
A program may use at most 192 MiB of HBM per device.

v0:
```python
import jax
import jax.numpy as jnp
from jax import lax
from jax.sharding import PartitionSpec as P

HEADS = 4
SCALE_POWER = -0.5


def shortened(array):
    return jax.tree.map(lambda a: a.astype(jnp.bfloat16) if a.dtype == jnp.float32 else a, array)


def shifted(value, axis, steps):
    count = lax.axis_size(axis)
    first, last = (max(0, -steps), min(count, count - steps))
    return lax.ppermute(value, axis, [(source, source + steps) for source in range(first, last)])


def with_halo(array, sides, width):
    for axis, dim in sides:
        peers, length = (lax.axis_size(axis), array.shape[dim])
        up = [(i, (i + 1) % peers) for i in range(peers - 1)]
        down = [(j, i) for i, j in up]
        last = lax.slice_in_dim(array, length - width, length, axis=dim)
        first = lax.slice_in_dim(array, 0, width, axis=dim)
        before = lax.ppermute(last, axis, up)
        after = lax.ppermute(first, axis, down)
        array = jnp.concatenate([before, array, after], axis=dim)
    return array


def product(pattern, first_op, second_op):
    return jnp.einsum(pattern, first_op, second_op, preferred_element_type=jnp.float32)


def stack_window(extended, tile_cols):
    window_parts = []
    for row_off in range(3):
        for col_off in range(3):
            window_parts.append(extended[row_off, col_off : col_off + tile_cols])
    stacked = jnp.stack(window_parts, axis=1)
    return stacked.reshape((tile_cols, 9 * stacked.shape[2]) + stacked.shape[3:])


def window_keep(row_ok, col_ok, tile_cols, tile_len):
    flag_list = []
    for row_off in range(3):
        for col_off in range(3):
            flag_list.append(
                jnp.logical_and(row_ok[row_off], col_ok[col_off : col_off + tile_cols])
            )
    stacked = jnp.stack(flag_list, axis=1)
    return jnp.repeat(stacked, tile_len, axis=1)


def spread_window(stacked, tile_cols, tile_len):
    window_parts = stacked.reshape((tile_cols, 3, 3, tile_len) + stacked.shape[2:])
    spread_rows = []
    for row_off in range(3):
        gathered = None
        for col_off in range(3):
            placed = jnp.pad(
                window_parts[:, row_off, col_off], ((col_off, 2 - col_off), (0, 0), (0, 0))
            )
            gathered = placed if gathered is None else gathered + placed
        spread_rows.append(gathered)
    return jnp.stack(spread_rows)


def widen_rim(edge_part, axis_pos, length, at_first):
    expanded = jnp.expand_dims(edge_part, axis_pos)
    pad_spec = [(0, 0)] * expanded.ndim
    pad_spec[axis_pos] = (0, length - 1) if at_first else (length - 1, 0)
    return jnp.pad(expanded, pad_spec)


def attend_row(query_row, key_ext, value_ext, visible, head_count):
    tile_cols, tile_len, feature_width = query_row.shape
    head_dim = feature_width // head_count
    score_scale = head_dim**SCALE_POWER
    query_heads = query_row.reshape(tile_cols, tile_len, head_count, head_dim)
    key_heads = stack_window(key_ext, tile_cols).reshape(
        tile_cols, 9 * tile_len, head_count, head_dim
    )
    value_heads = stack_window(value_ext, tile_cols).reshape(
        tile_cols, 9 * tile_len, head_count, head_dim
    )
    scores = product("jqhd,jkhd->jhqk", query_heads, key_heads) * score_scale
    scores = jnp.where(visible[:, None, None, :], scores, -1e30)
    row_max = jnp.max(scores, axis=-1, keepdims=True)
    log_norm = row_max + jnp.log(jnp.sum(jnp.exp(scores - row_max), axis=-1, keepdims=True))
    soft_probs = jnp.exp(scores - log_norm).astype(jnp.bfloat16)
    attended = product("jhqk,jkhd->jqhd", soft_probs, value_heads)
    attended = attended.reshape(tile_cols, tile_len, feature_width).astype(jnp.bfloat16)
    return (attended, soft_probs, log_norm[..., 0])


def query_back(query_row, key_ext, value_ext, attended, grad_attn, soft_probs, head_count):
    tile_cols, tile_len, feature_width = query_row.shape
    head_dim = feature_width // head_count
    score_scale = head_dim**SCALE_POWER
    attended_heads = attended.astype(jnp.float32).reshape(tile_cols, tile_len, head_count, head_dim)
    grad_heads = grad_attn.reshape(tile_cols, tile_len, head_count, head_dim)
    row_delta = jnp.sum(attended_heads * grad_heads.astype(jnp.float32), axis=-1)
    row_delta = jnp.transpose(row_delta, (0, 2, 1))
    value_heads = stack_window(value_ext, tile_cols).reshape(
        tile_cols, 9 * tile_len, head_count, head_dim
    )
    prob_grad = product("jqhd,jkhd->jhqk", grad_heads, value_heads)
    score_grad = (soft_probs.astype(jnp.float32) * (prob_grad - row_delta[..., None])).astype(
        jnp.bfloat16
    )
    key_heads = stack_window(key_ext, tile_cols).reshape(
        tile_cols, 9 * tile_len, head_count, head_dim
    )
    query_grad = product("jhqk,jkhd->jqhd", score_grad, key_heads) * score_scale
    query_grad = query_grad.reshape(tile_cols, tile_len, feature_width)
    query_heads = query_row.reshape(tile_cols, tile_len, head_count, head_dim)
    key_part = (product("jhqk,jqhd->jkhd", score_grad, query_heads) * score_scale).reshape(
        tile_cols, 9 * tile_len, feature_width
    )
    value_part = product("jhqk,jqhd->jkhd", soft_probs, grad_heads).reshape(
        tile_cols, 9 * tile_len, feature_width
    )
    return (
        query_grad,
        row_delta,
        spread_window(key_part, tile_cols, tile_len),
        spread_window(value_part, tile_cols, tile_len),
    )


def send_rows(edge_part, offset):
    return shifted(shortened(edge_part), "ha", offset).astype(edge_part.dtype)


def send_columns(edge_part, offset):
    return shifted(shortened(edge_part), "wa", offset).astype(edge_part.dtype)


def on_device(query_in, key_in, value_in, grad_out, out_weight):
    clip_count, tile_rows, tile_cols, tile_len, feature_width = query_in.shape
    model_width = grad_out.shape[-1]
    head_count = HEADS
    row_first = lax.axis_index("ha") * tile_rows
    col_first = lax.axis_index("wa") * tile_cols
    all_rows = tile_rows * lax.axis_size("ha")
    all_cols = tile_cols * lax.axis_size("wa")
    row_global = row_first - 1 + jnp.arange(tile_rows + 2, dtype=jnp.int32)
    row_flags = jnp.logical_and(row_global >= 0, row_global < all_rows)
    col_global = col_first - 1 + jnp.arange(tile_cols + 2, dtype=jnp.int32)
    col_ok = jnp.logical_and(col_global >= 0, col_global < all_cols)
    full_weight = lax.all_gather(out_weight, "dp", axis=0, tiled=True)
    flat_grad = grad_out.reshape(-1, model_width)
    grad_attn = lax.dot_general(
        flat_grad, full_weight, (((1,), (1,)), ((), ())), preferred_element_type=jnp.float32
    )
    grad_attn = grad_attn.astype(jnp.bfloat16).reshape(query_in.shape)
    extended = with_halo(jnp.stack([key_in, value_in]), (("ha", 2), ("wa", 3)), 1)
    key_ext_all = extended[0]
    value_ext_all = extended[1]
    row_total = clip_count * tile_rows
    flat_rows = jnp.arange(row_total, dtype=jnp.int32)
    query_rows = query_in.reshape(row_total, tile_cols, tile_len, feature_width)
    grad_rows = grad_attn.reshape(row_total, tile_cols, tile_len, feature_width)

    def row_window(extended_all):
        return extended_all[0]

    def row_keep():
        return window_keep(row_flags, col_ok, tile_cols, tile_len)

    def forward_row(inputs):
        query_row, flat_index = inputs
        return attend_row(
            query_row, row_window(key_ext_all), row_window(value_ext_all), row_keep(), head_count
        )

    attended, soft_probs, log_norm = lax.map(forward_row, (query_rows, flat_rows))
    flat_attn = attended.reshape(-1, feature_width)
    outcome = jnp.dot(flat_attn, full_weight, preferred_element_type=jnp.float32).astype(
        jnp.bfloat16
    )
    outcome = outcome.reshape(clip_count, tile_rows, tile_cols, tile_len, model_width)

    def query_side(inputs):
        query_row, grad_row, attended_row, probs_row, flat_index = inputs
        query_grad, row_delta, key_part, value_part = query_back(
            query_row,
            row_window(key_ext_all),
            row_window(value_ext_all),
            attended_row,
            grad_row,
            probs_row,
            head_count,
        )
        return (query_grad, jnp.stack([key_part, value_part]))

    query_grad, ext_parts = lax.map(
        query_side, (query_rows, grad_rows, attended, soft_probs, flat_rows)
    )
    ext_parts = ext_parts.reshape(
        clip_count, tile_rows, 2, 3, tile_cols + 2, tile_len, feature_width
    )
    padded_grad = None
    for row_off in range(3):
        placed = jnp.pad(
            ext_parts[:, :, :, row_off],
            ((0, 0), (row_off, 2 - row_off), (0, 0), (0, 0), (0, 0), (0, 0)),
        )
        padded_grad = placed if padded_grad is None else padded_grad + placed
    from_below = send_rows(padded_grad[:, 0], -1)
    from_above = send_rows(padded_grad[:, tile_rows + 1], 1)
    middle = padded_grad[:, 1 : tile_rows + 1]
    middle = (
        middle
        + widen_rim(from_below, 1, tile_rows, False)
        + widen_rim(from_above, 1, tile_rows, True)
    )
    from_right = send_columns(middle[:, :, :, 0], -1)
    from_left = send_columns(middle[:, :, :, tile_cols + 1], 1)
    core_part = middle[:, :, :, 1 : tile_cols + 1]
    core_part = (
        core_part
        + widen_rim(from_right, 3, tile_cols, False)
        + widen_rim(from_left, 3, tile_cols, True)
    )
    key_grad = core_part[:, :, 0]
    value_grad = core_part[:, :, 1]
    query_grad = query_grad.reshape(query_in.shape)
    row_share = feature_width // lax.axis_size("dp")
    local_term = lax.dot_general(
        flat_attn, flat_grad, (((0,), (0,)), ((), ())), preferred_element_type=jnp.float32
    )
    summed = lax.psum(local_term, ("dp", "ha", "wa"))
    weight_grad = lax.dynamic_slice_in_dim(summed, lax.axis_index("dp") * row_share, row_share, 0)
    return (outcome, query_grad, key_grad, value_grad, weight_grad)


def solution(mesh):
    return jax.shard_map(
        on_device,
        mesh=mesh,
        in_specs=(
            P("dp", "ha", "wa", None, None),
            P("dp", "ha", "wa", None, None),
            P("dp", "ha", "wa", None, None),
            P("dp", "ha", "wa", None, None),
            P("dp", None),
        ),
        out_specs=(
            P("dp", "ha", "wa", None, None),
            P("dp", "ha", "wa", None, None),
            P("dp", "ha", "wa", None, None),
            P("dp", "ha", "wa", None, None),
            P("dp", None),
        ),
        check_vma=False,
    )
```

profile of v0, /device:TPU:0, one launch (start us, length us, event | category | flops | bytes accessed | tf_op | source)
XLA Modules:
  0.0 480.3 jit_solution(6171080770053422806)
XLA Ops:
  10.5 5.6 %collective-permute-start = (bf16[2,1,1,1,384,512]{5,4,3,2,1,0:T(8,128)(2,1)S(1)}, bf16[2,1,1,1,384,512]{5,4,3,2,1,0:T(8,128)(2,1)S(1)}, u32[]{:S(2)}, u32[]{:S(2)}) collective-permute-start(bf16[2,1,1,1,384,512]{5,4,3,2,1,0:T(8,128)(2,1)S(1)} %pad_maximum_fusion.4), channel_id=1, source_target_pairs={{0,4},{4,8},{8,12},{1,5},{5,9},{9,13},{2,6},{6,10},{10,14},{3,7},{... | collective-permute-start | bytes 2359304 | tf_op jit(solution)/shard_map/ppermute | solution.py:27
  16.1 15.6 %collective-permute-done.1 = bf16[2,1,1,1,384,512]{5,4,3,2,1,0:T(8,128)(2,1)S(1)} collective-permute-done((bf16[2,1,1,1,384,512]{5,4,3,2,1,0:T(8,128)(2,1)S(1)}, bf16[2,1,1,1,384,512]{5,4,3,2,1,0:T(8,128)(2,1)S(1)}, u32[]{:S(2)}, u32[]{:S(2)}) %collective-permute-start.1) | collective-permute-done | bytes 786464 | tf_op jit(solution)/shard_map/ppermute | solution.py:28
  32.9 3.1 pad_maximum_fusion.3
  37.2 4.5 collective-permute-start.2
  54.9 2.3 all-gather.2.cloned.1.call-done
  57.2 3.3 fusion.17
  63.6 3.8 pad_maximum_fusion
  67.3 2.1 slice_bitcast_fusion.12
  69.5 2.0 pad_maximum_fusion.2
  71.5 7.2 %reshape.242 = bf16[3456,4,128]{2,1,0:T(4,128)(2,1)} reshape(bf16[1,9,384,512]{3,2,1,0:T(8,128)(2,1)} %pad_maximum_fusion.2) | data formatting | bytes 7077888 | tf_op jit(solution)/shard_map/reshape.31
  78.7 6.9 %copy.102 = bf16[3456,4,128]{0,2,1:T(8,128)(2,1)} copy(bf16[3456,4,128]{2,1,0:T(4,128)(2,1)} %reshape.242) | data formatting | bytes 7077888 | tf_op jit(solution)/shard_map/reshape.31
  85.6 7.5 %bitcast_reduce_fusion = (f32[4,384]{1,0:T(4,128)S(1)}, f32[4,3456,384]{2,1,0:T(8,128)S(1)}) fusion(pred[3456]{0:T(1024)(128)(4,1)S(1)} %broadcast_in_dim.69, bf16[3456,4,128]{0,2,1:T(8,128)(2,1)} %copy.102, bf16[384,4,128]{2,1,0:T(4,128)(2,1)S(1)} %copy-done.9), kind=kOutput, calls=%fused_computation.2 | convolution fusion | flops 1374878208 | bytes 25175424 | tf_op jit(solution)/shard_map/while/body/eval_jaxpr/jqhd,jkhd->jhqk/dot_general | solution.py:34
  93.1 5.7 %fusion.1 = f32[4,384]{1,0:T(4,128)S(1)} fusion(f32[4,3456,384]{2,1,0:T(8,128)S(1)} %get-tuple-element.125, f32[4,384]{1,0:T(4,128)S(1)} %get-tuple-element.124, pred[3456]{0:T(1024)(128)(4,1)S(1)} %broadcast_in_dim.69), kind=kLoop, calls=%fused_computation.4 | loop fusion | flops 21232128 | bytes 21249408 | tf_op jit(solution)/shard_map/while/body/eval_jaxpr/reduce_sum | solution.py:92
  98.8 7.5 %fusion.3 = bf16[4,384,3456]{1,2,0:T(8,128)(2,1)} fusion(f32[4,3456,384]{2,1,0:T(8,128)S(1)} %get-tuple-element.125, f32[4,384]{1,0:T(4,128)S(1)} %log_add_fusion, pred[3456]{0:T(1024)(128)(4,1)S(1)} %broadcast_in_dim.69), kind=kLoop, calls=%fused_computation.6 | loop fusion | flops 21233664 | bytes 31860096 | tf_op jit(solution)/shard_map/while/body/eval_jaxpr/convert_element_type | solution.py:93
  108.2 7.4 %reshape.241 = bf16[3456,4,128]{2,1,0:T(4,128)(2,1)} reshape(bf16[1,9,384,512]{3,2,1,0:T(8,128)(2,1)} %pad_maximum_fusion.1) | data formatting | bytes 7077888 | tf_op jit(solution)/shard_map/reshape.41
  115.6 10.2 %convolution_bitcast_fusion = f32[1,3456,4,128]{1,3,2,0:T(8,128)} fusion(bf16[384,4,128]{0,2,1:T(8,128)(2,1)S(1)} %bitcast.185, bf16[4,384,3456]{1,2,0:T(8,128)(2,1)} %fusion.3), kind=kOutput, calls=%fused_computation.15 | convolution fusion | flops 1358954496 | bytes 18087936 | tf_op jit(solution)/shard_map/while/body/eval_jaxpr/jhqk,jqhd->jkhd/dot_general | solution.py:34
  125.8 6.3 %multiply_reduce_fusion = (f32[384,4]{0,1:T(4,128)S(1)}, bf16[4,128,384]{2,1,0:T(8,128)(2,1)S(1)}) fusion(f32[1,384,4,128]{1,3,2,0:T(8,128)S(1)} %bitcast.195, bf16[4,384,3456]{1,2,0:T(8,128)(2,1)} %fusion.3, bf16[3456,4,128]{2,1,0:T(4,128)(2,1)S(1)} %copy-done.2), kind=kOutput, calls=%fused_computation.75 | convolution fusion | flops 1359739392 | bytes 15341568 | tf_op jit(solution)/shard_map/while/body/eval_jaxpr/jhqk,jkhd->jqhd/dot_general | solution.py:34
  132.1 12.1 %multiply_convert_fusion = bf16[4,384,3456]{1,2,0:T(8,128)(2,1)} fusion(bf16[4,384,3456]{1,2,0:T(8,128)(2,1)} %fusion.3, bf16[384,4,128]{0,2,1:T(8,128)(2,1)S(1)} %bitcast.186, f32[4,384]{1,0:T(4,128)S(1)} %bitcast.197, bf16[3456,4,128]{2,1,0:T(4,128)(2,1)} %reshape.241), kind=kOutput, calls=%fused_computation.7 | convolution fusion | flops 1380188160 | bytes 25171968 | tf_op jit(solution)/shard_map/while/body/eval_jaxpr/jqhd,jkhd->jhqk/dot_general | solution.py:34
  144.2 9.2 %copy.108 = f32[1,3456,4,128]{3,2,0,1:T(4,128)} copy(f32[1,3456,4,128]{1,3,2,0:T(8,128)} %convolution_bitcast_fusion) | data formatting | bytes 14155776 | tf_op jit(solution)/shard_map/while/body/eval_jaxpr/jhqk,jqhd->jkhd/transpose | solution.py:34
  153.4 8.4 %slice_bitcast_fusion.23 = (f32[1,384,512]{2,0,1:T(1,128)S(1)}, f32[1,384,512]{2,0,1:T(1,128)}, f32[1,384,512]{2,0,1:T(1,128)}, f32[1,384,512]{2,0,1:T(1,128)}, ...) fusion(f32[1,3,3,384,512]{4,0,3,2,1:T(1,128)} %bitcast.183), kind=kLoop, calls=%fused_computation.64 | loop fusion | bytes 14155776 | tf_op jit(solution)/shard_map/while/body/eval_jaxpr/squeeze | solution.py:64
  161.8 2.9 multiply_bitcast_fusion
  164.7 15.1 %copy.105 = f32[1,3456,4,128]{3,2,0,1:T(4,128)S(1)} copy(f32[1,3456,4,128]{3,1,2,0:T(8,128)S(1)} %multiply_bitcast_fusion) | data formatting | bytes 14155776 | tf_op jit(solution)/shard_map/while/body/eval_jaxpr/mul | solution.py:120
  179.8 4.1 slice_bitcast_fusion.32
  184.0 3.2 add_bitcast_fusion
  187.2 3.2 add_bitcast_fusion.1
  190.4 3.2 add_bitcast_fusion.2
  193.5 9.7 %maximum_bitcast_fusion.2 = f32[1,3,3,384,512]{4,2,3,1,0:T(4,128)} fusion(f32[1,3,384,512]{3,1,2,0:T(4,128)} %add_bitcast_fusion, f32[1,3,384,512]{3,1,2,0:T(4,128)} %add_bitcast_fusion.1, f32[1,3,384,512]{3,1,2,0:T(4,128)} %add_bitcast_fusion.2), kind=kLoop, calls=%fused_computation.12 | loop fusion | flops 3538944 | bytes 14155776 | tf_op jit(solution)/shard_map/while/body/eval_jaxpr/stack | solution.py:198
  203.2 4.5 add_bitcast_fusion.3
  207.8 3.6 add_bitcast_fusion.4
  211.3 3.2 add_bitcast_fusion.5
  214.5 9.7 %maximum_bitcast_fusion.1 = f32[1,3,3,384,512]{4,2,3,1,0:T(4,128)} fusion(f32[1,3,384,512]{3,1,2,0:T(4,128)} %add_bitcast_fusion.3, f32[1,3,384,512]{3,1,2,0:T(4,128)} %add_bitcast_fusion.4, f32[1,3,384,512]{3,1,2,0:T(4,128)} %add_bitcast_fusion.5), kind=kLoop, calls=%fused_computation.11 | loop fusion | flops 3538944 | bytes 14155776 | tf_op jit(solution)/shard_map/while/body/eval_jaxpr/stack | solution.py:198
  224.2 10.5 %maximum_bitcast_fusion = f32[1,1,2,3,3,384,512]{6,4,5,3,2,1,0:T(4,128)S(1)} fusion(f32[1,3,3,384,512]{4,2,3,1,0:T(4,128)} %maximum_bitcast_fusion.2, f32[1,3,3,384,512]{4,2,3,1,0:T(4,128)} %maximum_bitcast_fusion.1), kind=kLoop, calls=%fused_computation.9 | loop fusion | flops 3538944 | bytes 28311552 | tf_op jit(solution)/shard_map/reshape | solution.py:203
  234.6 7.7 %slice_bitcast_fusion.2 = (f32[1,1,2,3,384,512]{5,3,4,2,1,0:T(4,128)}, f32[1,1,2,3,384,512]{5,3,4,2,1,0:T(4,128)}, f32[1,1,2,3,384,512]{5,3,4,2,1,0:T(4,128)}) fusion(f32[1,1,2,3,3,384,512]{6,4,5,3,2,1,0:T(4,128)S(1)} %maximum_bitcast_fusion), kind=kLoop, calls=%fused_computation.20 | loop fusion | bytes 28311552 | tf_op jit(solution)/shard_map/squeeze | solution.py:209
  242.3 18.2 %pad_add_fusion = (f32[1,3,2,3,384,512]{5,3,4,2,1,0:T(4,128)}, bf16[1,3,2,3,384,512]{5,3,4,2,1,0:T(4,128)(2,1)S(1)}) fusion(f32[1,1,2,3,384,512]{5,3,4,2,1,0:T(4,128)} %get-tuple-element.86, f32[1,1,2,3,384,512]{5,3,4,2,1,0:T(4,128)} %get-tuple-element.87, f32[1,1,2,3,384,512]{5,3,4,2,1,0:T(4,128)} %get-tuple-element.85), kind=kLoop, calls=%fused_computation.10 | loop fusion | flops 10616832 | bytes 35389440 | tf_op jit(solution)/shard_map/add | solution.py:212
  260.6 2.2 slice_bitcast_fusion.4
  264.8 4.8 collective-permute-start.5
  272.8 4.4 fusion.9
  277.2 63.5 %collective-permute-done.5 = bf16[1,2,3,384,512]{4,3,2,1,0:T(8,128)(2,1)} collective-permute-done((bf16[1,2,3,384,512]{4,3,2,1,0:T(8,128)(2,1)}, bf16[1,2,3,384,512]{4,3,2,1,0:T(8,128)(2,1)}, u32[]{:S(2)}, u32[]{:S(2)}) %collective-permute-start.5) | collective-permute-done | bytes 2359328 | tf_op jit(solution)/shard_map/ppermute | solution.py:17
  340.7 12.7 %collective-permute-done.4 = bf16[1,2,3,384,512]{4,3,2,1,0:T(8,128)(2,1)} collective-permute-done((bf16[1,2,3,384,512]{4,3,2,1,0:T(8,128)(2,1)}, bf16[1,2,3,384,512]{4,3,2,1,0:T(8,128)(2,1)}, u32[]{:S(2)}, u32[]{:S(2)}) %collective-permute-start.4) | collective-permute-done | bytes 2359328 | tf_op jit(solution)/shard_map/ppermute | solution.py:17
  353.5 10.7 %fusion.24 = (bf16[1,1,2,3,384,512]{5,3,4,2,1,0:T(4,128)(2,1)S(1)}, f32[1,1,2,3,384,512]{5,3,4,2,1,0:T(4,128)}) fusion(bf16[1,2,3,384,512]{4,3,2,1,0:T(8,128)(2,1)} %collective-permute-done.5, bf16[1,2,3,384,512]{4,3,2,1,0:T(8,128)(2,1)} %collective-permute-done.4, f32[1,3,2,3,384,512]{5,3,4,2,1,0:T(4,128)} %get-tuple-element.83), kind=kLoop, calls=%fused_computation.84 | loop fusion | flops 5898240 | bytes 16515072 | tf_op jit(solution)/shard_map/convert.6
  364.2 3.4 slice_bitcast_fusion.6
  367.6 6.8 %collective-permute-start.7 = (bf16[1,1,2,384,512]{4,0,3,2,1:T(2,128)(2,1)}, bf16[1,1,2,384,512]{4,0,3,2,1:T(2,128)(2,1)}, u32[]{:S(2)}, u32[]{:S(2)}) collective-permute-start(bf16[1,1,2,384,512]{4,0,3,2,1:T(2,128)(2,1)} %get-tuple-element.115), channel_id=1, source_target_pairs={{0,1},{1,2},{2,3},{4,5},{5,6},{6,7},{8,9},{9,10},{10,11},{12,13},{... | collective-permute-start | bytes 2359304 | tf_op jit(solution)/shard_map/ppermute | solution.py:17
  375.7 7.2 %convolution_multiply_fusion = f32[4,128,384]{2,1,0:T(8,128)} fusion(bf16[3456,4,128]{0,2,1:T(8,128)(2,1)S(1)} %copy-done.3, bf16[4,384,3456]{1,2,0:T(8,128)(2,1)} %multiply_convert_fusion), kind=kOutput, calls=%fused_computation.45 | convolution fusion | flops 1359151104 | bytes 14942208 | tf_op jit(solution)/shard_map/while/body/eval_jaxpr/jhqk,jkhd->jqhd/dot_general | solution.py:34
  382.9 2.3 copy.117
  385.2 4.7 fusion.5
  389.9 7.0 %fusion.13 = f32[1,1,2,1,384,512]{5,3,4,2,1,0:T(1,128)S(1)} fusion(f32[1,1,2,3,384,512]{5,3,4,2,1,0:T(4,128)} %get-tuple-element.82, bf16[1,1,2,384,512]{4,0,3,2,1:T(2,128)(2,1)} %collective-permute-done.7, bf16[1,1,2,384,512]{4,0,3,2,1:T(2,128)(2,1)} %collective-permute-done.6), kind=kLoop, calls=%fused_computation.44 | loop fusion | flops 1572864 | bytes 4718592 | tf_op jit(solution)/shard_map/add | solution.py:225
  399.9 69.5 %all-reduce.23.cloned.1.call-done = f32[512,3072]{1,0:T(8,128)} async-done(((f32[512,3072]{1,0:T(8,128)}), f32[512,3072]{1,0:T(8,128)}) %all-reduce.23.cloned.1.call-update) | async-done | bytes 6291472 | tf_op jit(solution)/shard_map/psum | solution.py:236
  469.4 3.9 constant_dynamic-slice_fusion
  (82 shorter events, 22.1 us)
Async XLA Ops:
  7.2 50.0 %copy-start = (bf16[1,1,1,384,3072]{4,3,2,1,0:T(8,128)(2,1)S(1)}, bf16[1,1,1,384,3072]{4,3,2,1,0:T(8,128)(2,1)}, u32[]{:S(2)}) copy-start(bf16[1,1,1,384,3072]{4,3,2,1,0:T(8,128)(2,1)} %param.8) | copy-start | bytes 7077892
  7.2 50.0 %all-gather.2.cloned.1.call-start = ((), (), s32[]{:S(2)}) async-start(), calls=%async_computation | async-start | bytes 4718592 | tf_op jit(solution)/shard_map/all_gather | solution.py:154
  7.9 46.0 %copy-start.25 = (bf16[1,1,1,384,512]{4,3,2,1,0:T(8,128)(2,1)S(1)}, bf16[1,1,1,384,512]{4,3,2,1,0:T(8,128)(2,1)}, u32[]{:S(2)}) copy-start(bf16[1,1,1,384,512]{4,3,2,1,0:T(8,128)(2,1)} %param.5) | copy-start | bytes 1179652
  7.9 461.5 %all-reduce.23.cloned.1.call-start = ((), (), s32[]{:S(2)}) async-start(), calls=%async_computation.1 | async-start | bytes 12582912 | tf_op jit(solution)/shard_map/psum | solution.py:236
  9.2 22.5 %collective-permute-start.1 = (bf16[2,1,1,1,384,512]{5,4,3,2,1,0:T(8,128)(2,1)S(1)}, bf16[2,1,1,1,384,512]{5,4,3,2,1,0:T(8,128)(2,1)S(1)}, u32[]{:S(2)}, u32[]{:S(2)}) collective-permute-start(bf16[2,1,1,1,384,512]{5,4,3,2,1,0:T(8,128)(2,1)S(1)} %pad_maximum_fusion.4), channel_id=1, source_target_pairs={{4,0},{8,4},{12,8},{5,1},{9,5},{13,9},{6,2},{10,6},{14,10},{7,3},{... | collective-permute-start | bytes 2359304 | tf_op jit(solution)/shard_map/ppermute | solution.py:28
  10.5 22.4 %collective-permute-start = (bf16[2,1,1,1,384,512]{5,4,3,2,1,0:T(8,128)(2,1)S(1)}, bf16[2,1,1,1,384,512]{5,4,3,2,1,0:T(8,128)(2,1)S(1)}, u32[]{:S(2)}, u32[]{:S(2)}) collective-permute-start(bf16[2,1,1,1,384,512]{5,4,3,2,1,0:T(8,128)(2,1)S(1)} %pad_maximum_fusion.4), channel_id=1, source_target_pairs={{0,4},{4,8},{8,12},{1,5},{5,9},{9,13},{2,6},{6,10},{10,14},{3,7},{... | collective-permute-start | bytes 2359304 | tf_op jit(solution)/shard_map/ppermute | solution.py:27
  31.7 1.2 copy-start.11
  32.9 3.1 copy-start.12
  35.9 27.6 %collective-permute-start.3 = (bf16[2,1,3,1,384,512]{5,4,3,2,1,0:T(8,128)(2,1)}, bf16[2,1,3,1,384,512]{5,4,3,2,1,0:T(8,128)(2,1)}, u32[]{:S(2)}, u32[]{:S(2)}) collective-permute-start(bf16[2,1,3,1,384,512]{5,4,3,2,1,0:T(8,128)(2,1)} %pad_maximum_fusion.3), channel_id=1, source_target_pairs={{1,0},{2,1},{3,2},{5,4},{6,5},{7,6},{9,8},{10,9},{11,10},{13,12},{... | collective-permute-start | bytes 7077896 | tf_op jit(solution)/shard_map/ppermute | solution.py:28
  37.2 26.3 %collective-permute-start.2 = (bf16[2,1,3,1,384,512]{5,4,3,2,1,0:T(8,128)(2,1)}, bf16[2,1,3,1,384,512]{5,4,3,2,1,0:T(8,128)(2,1)}, u32[]{:S(2)}, u32[]{:S(2)}) collective-permute-start(bf16[2,1,3,1,384,512]{5,4,3,2,1,0:T(8,128)(2,1)} %pad_maximum_fusion.3), channel_id=1, source_target_pairs={{0,1},{1,2},{2,3},{4,5},{5,6},{6,7},{8,9},{9,10},{10,11},{12,13},{... | collective-permute-start | bytes 7077896 | tf_op jit(solution)/shard_map/ppermute | solution.py:27
  54.9 8.7 %copy-start.7 = (bf16[1,1,1,384,512]{4,3,2,1,0:T(8,128)(2,1)S(1)}, bf16[1,1,1,384,512]{4,3,2,1,0:T(8,128)(2,1)}, u32[]{:S(2)}) copy-start(bf16[1,1,1,384,512]{4,3,2,1,0:T(8,128)(2,1)} %param.7) | copy-start | bytes 1179652
  54.9 8.7 %copy-start.8 = (bf16[1,1,1,384,512]{4,3,2,1,0:T(8,128)(2,1)S(1)}, bf16[1,1,1,384,512]{4,3,2,1,0:T(8,128)(2,1)}, u32[]{:S(2)}) copy-start(bf16[1,1,1,384,512]{4,3,2,1,0:T(8,128)(2,1)} %param.6) | copy-start | bytes 1179652
  60.5 0.7 copy-start.24
  78.7 6.9 %copy-start.9 = (bf16[384,4,128]{2,1,0:T(4,128)(2,1)S(1)}, bf16[384,4,128]{2,1,0:T(4,128)(2,1)}, u32[]{:S(2)}) copy-start(bf16[384,4,128]{2,1,0:T(4,128)(2,1)} %reshape.243) | copy-start | bytes 1179652
  98.7 7.5 %copy-start.4 = (bf16[1,3,384,512]{3,2,1,0:T(8,128)(2,1)S(1)}, bf16[1,3,384,512]{3,2,1,0:T(8,128)(2,1)}, u32[]{:S(2)}) copy-start(bf16[1,3,384,512]{3,2,1,0:T(8,128)(2,1)} %get-tuple-element.108) | copy-start | bytes 3538948
  98.8 7.5 %copy-start.5 = (bf16[1,3,384,512]{3,2,1,0:T(8,128)(2,1)S(1)}, bf16[1,3,384,512]{3,2,1,0:T(8,128)(2,1)}, u32[]{:S(2)}) copy-start(bf16[1,3,384,512]{3,2,1,0:T(8,128)(2,1)} %get-tuple-element.112) | copy-start | bytes 3538948
  98.8 7.5 %copy-start.6 = (bf16[1,3,384,512]{3,2,1,0:T(8,128)(2,1)S(1)}, bf16[1,3,384,512]{3,2,1,0:T(8,128)(2,1)}, u32[]{:S(2)}) copy-start(bf16[1,3,384,512]{3,2,1,0:T(8,128)(2,1)} %get-tuple-element.113) | copy-start | bytes 3538948
  115.6 10.2 %copy-start.2 = (bf16[3456,4,128]{2,1,0:T(4,128)(2,1)S(1)}, bf16[3456,4,128]{2,1,0:T(4,128)(2,1)}, u32[]{:S(2)}) copy-start(bf16[3456,4,128]{2,1,0:T(4,128)(2,1)} %reshape.241) | copy-start | bytes 10616836
  115.6 10.2 %copy-start.10 = (f32[384,512]{0,1:T(8,128)S(1)}, f32[384,512]{0,1:T(8,128)}, u32[]{:S(2)}) copy-start(f32[384,512]{0,1:T(8,128)} %copy.100) | copy-start | bytes 2359300
  153.4 8.4 %copy-start.1 = (bf16[4,384,3456]{1,2,0:T(8,128)(2,1)S(1)}, bf16[4,384,3456]{1,2,0:T(8,128)(2,1)}, u32[]{:S(2)}) copy-start(bf16[4,384,3456]{1,2,0:T(8,128)(2,1)} %multiply_convert_fusion) | copy-start | bytes 31850500
  179.8 4.2 copy-start.21
  179.8 4.2 copy-start.22
  179.8 4.2 copy-start.23
  184.0 3.2 copy-start.19
  184.0 3.2 copy-start.20
  203.2 4.5 copy-start.16
  203.2 4.5 copy-start.17
  203.2 4.5 copy-start.18
  207.7 3.6 copy-start.13
  207.7 3.6 copy-start.14
  207.7 3.6 copy-start.15
  264.8 76.0 %collective-permute-start.5 = (bf16[1,2,3,384,512]{4,3,2,1,0:T(8,128)(2,1)}, bf16[1,2,3,384,512]{4,3,2,1,0:T(8,128)(2,1)}, u32[]{:S(2)}, u32[]{:S(2)}) collective-permute-start(bf16[1,2,3,384,512]{4,3,2,1,0:T(8,128)(2,1)} %copy.113), channel_id=1, source_target_pairs={{0,4},{4,8},{8,12},{1,5},{5,9},{9,13},{2,6},{6,10},{10,14},{3,7},{... | collective-permute-start | bytes 7077896 | tf_op jit(solution)/shard_map/ppermute | solution.py:17
  271.5 82.0 %collective-permute-start.4 = (bf16[1,2,3,384,512]{4,3,2,1,0:T(8,128)(2,1)}, bf16[1,2,3,384,512]{4,3,2,1,0:T(8,128)(2,1)}, u32[]{:S(2)}, u32[]{:S(2)}) collective-permute-start(bf16[1,2,3,384,512]{4,3,2,1,0:T(8,128)(2,1)} %copy.111), channel_id=1, source_target_pairs={{4,0},{8,4},{12,8},{5,1},{9,5},{13,9},{6,2},{10,6},{14,10},{7,3},{... | collective-permute-start | bytes 7077896 | tf_op jit(solution)/shard_map/ppermute | solution.py:17
  364.2 11.5 %copy-start.3 = (bf16[3456,4,128]{0,2,1:T(8,128)(2,1)S(1)}, bf16[3456,4,128]{0,2,1:T(8,128)(2,1)}, u32[]{:S(2)}) copy-start(bf16[3456,4,128]{0,2,1:T(8,128)(2,1)} %copy.102) | copy-start | bytes 10616836
  367.6 22.3 %collective-permute-start.7 = (bf16[1,1,2,384,512]{4,0,3,2,1:T(2,128)(2,1)}, bf16[1,1,2,384,512]{4,0,3,2,1:T(2,128)(2,1)}, u32[]{:S(2)}, u32[]{:S(2)}) collective-permute-start(bf16[1,1,2,384,512]{4,0,3,2,1:T(2,128)(2,1)} %get-tuple-element.115), channel_id=1, source_target_pairs={{0,1},{1,2},{2,3},{4,5},{5,6},{6,7},{8,9},{9,10},{10,11},{12,13},{... | collective-permute-start | bytes 2359304 | tf_op jit(solution)/shard_map/ppermute | solution.py:17
  374.4 15.5 %collective-permute-start.6 = (bf16[1,1,2,384,512]{4,0,3,2,1:T(2,128)(2,1)}, bf16[1,1,2,384,512]{4,0,3,2,1:T(2,128)(2,1)}, u32[]{:S(2)}, u32[]{:S(2)}) collective-permute-start(bf16[1,1,2,384,512]{4,0,3,2,1:T(2,128)(2,1)} %get-tuple-element.114), channel_id=1, source_target_pairs={{1,0},{2,1},{3,2},{5,4},{6,5},{7,6},{9,8},{10,9},{11,10},{13,12},{... | collective-permute-start | bytes 2359304 | tf_op jit(solution)/shard_map/ppermute | solution.py:17
Sparse Core Ops, SparseCore 0:
  9.5 47.6 all-gather.1
  277.4 191.9 all-reduce.22
where the time goes:
time: 490 us; the launch traced here: 480 us
  waiting for transfers between devices  166 us (34%)
  other arithmetic  112 us (23%)
  local copies, waits for them, and re-layouts  91.6 us (19%)
  matrix products  58.7 us (12%)
  starting transfers between devices  26.9 us (5%)
  between operations  26 us (5%)
    ppermute x4, waiting for transfers between devices, shifted(): lax.ppermute(value, axis, [(source, source + steps) for source in range(f...  76.2 us
    psum x1, waiting for transfers between devices, on_device(): summed = lax.psum(local_term, ('dp', 'ha', 'wa'))  69.5 us
    dot_general x6, matrix products, product(): jnp.einsum(pattern, first_op, second_op, preferred_element_type=jnp.float32)  46.2 us
    another operation x5, local copies, waits for them, and re-layouts  23.5 us
    another operation x6, other arithmetic, spread_window(): return jnp.stack(spread_rows)  20.8 us
    another operation x2, other arithmetic, query_side(): return (query_grad, jnp.stack([key_part, value_part]))  19.3 us
    add x1, other arithmetic, on_device(): padded_grad = placed if padded_grad is None else padded_grad + placed  18.2 us
    ppermute x2, waiting for transfers between devices, with_halo(): after = lax.ppermute(first, axis, down)  15.6 us
  transfers between devices with their start and end apart: 10, of which 6 were waited for; matrix products, arithmetic and copies ran while one was open for 12% of the time, Pallas kernels for 0%

commit v1 on v0

--- a/solution.py
+++ b/solution.py
@@ -233,7 +233,9 @@
     local_term = lax.dot_general(
         flat_attn, flat_grad, (((0,), (0,)), ((), ())), preferred_element_type=jnp.float32
     )
-    summed = lax.psum(local_term, ("dp", "ha", "wa"))
+    summed = local_term
+    for it in ("dp", ("ha", "wa")):
+        summed = lax.psum(summed, it)
     weight_grad = lax.dynamic_slice_in_dim(summed, lax.axis_index("dp") * row_share, row_share, 0)
     return (outcome, query_grad, key_grad, value_grad, weight_grad)
 

time: 490 us -> 522 us (1.065)
  waiting for transfers between devices: 166 us -> 191 us
  local copies, waits for them, and re-layouts: 91.6 us -> 104 us
  starting transfers between devices: 26.9 us -> 20.8 us
    psum x1 -> x2, waiting for transfers between devices: 69.5 us -> 171 us  [on_device(): summed = lax.psum(summed, it)]
    ppermute x4, waiting for transfers between devices: 76.2 us -> 0.01 us  [shifted(): lax.ppermute(value, axis, [(source, source + steps) for source in range(f...]
    mul x1, local copies, waits for them, and re-layouts: 15.1 us -> 25.5 us  [query_back(): product('jhqk,jqhd->jkhd', score_grad, query_heads) * score_scale]
    ppermute x4, starting transfers between devices: 14.1 us -> 8.01 us  [shifted(): lax.ppermute(value, axis, [(source, source + steps) for source in range(f...]
  transfers between devices with their start and end apart: 10 -> 11, of which waited for: 6 -> 5; matrix products, arithmetic and copies ran while one was open for 12% -> 26% of each run, Pallas kernels for 0% -> 0%
where the time goes in v1:
time: 522 us; the launch traced here: 513 us
  waiting for transfers between devices  191 us (37%)
  other arithmetic  114 us (22%)
  local copies, waits for them, and re-layouts  104 us (20%)
  matrix products  57.9 us (11%)
  between operations  26 us (5%)
  starting transfers between devices  20.8 us (4%)
    psum x2, waiting for transfers between devices, on_device(): summed = lax.psum(summed, it)  171 us
    dot_general x6, matrix products, product(): jnp.einsum(pattern, first_op, second_op, preferred_element_type=jnp.float32)  45.4 us
    mul x1, local copies, waits for them, and re-layouts, query_back(): product('jhqk,jqhd->jkhd', score_grad, query_heads) * score_scale  25.5 us
    another operation x5, local copies, waits for them, and re-layouts  23.6 us
    another operation x2, other arithmetic, query_side(): return (query_grad, jnp.stack([key_part, value_part]))  21 us
    another operation x6, other arithmetic, spread_window(): return jnp.stack(spread_rows)  19 us
    add x1, other arithmetic, on_device(): padded_grad = placed if padded_grad is None else padded_grad + placed  18.3 us
    ppermute x2, waiting for transfers between devices, with_halo(): after = lax.ppermute(first, axis, down)  15.6 us
  transfers between devices with their start and end apart: 11, of which 5 were waited for; matrix products, arithmetic and copies ran while one was open for 26% of the time, Pallas kernels for 0%

profile of v1, /device:TPU:0, one launch (start us, length us, event | category | flops | bytes accessed | tf_op | source)
XLA Modules:
  0.0 513.1 jit_solution(16395398986275499475)
XLA Ops:
  10.5 5.6 %collective-permute-start = (bf16[2,1,1,1,384,512]{5,4,3,2,1,0:T(8,128)(2,1)S(1)}, bf16[2,1,1,1,384,512]{5,4,3,2,1,0:T(8,128)(2,1)S(1)}, u32[]{:S(2)}, u32[]{:S(2)}) collective-permute-start(bf16[2,1,1,1,384,512]{5,4,3,2,1,0:T(8,128)(2,1)S(1)} %pad_maximum_fusion.4), channel_id=1, source_target_pairs={{0,4},{4,8},{8,12},{1,5},{5,9},{9,13},{2,6},{6,10},{10,14},{3,7},{... | collective-permute-start | bytes 2359304 | tf_op jit(solution)/shard_map/ppermute | solution.py:27
  16.1 15.6 %collective-permute-done.1 = bf16[2,1,1,1,384,512]{5,4,3,2,1,0:T(8,128)(2,1)S(1)} collective-permute-done((bf16[2,1,1,1,384,512]{5,4,3,2,1,0:T(8,128)(2,1)S(1)}, bf16[2,1,1,1,384,512]{5,4,3,2,1,0:T(8,128)(2,1)S(1)}, u32[]{:S(2)}, u32[]{:S(2)}) %collective-permute-start.1) | collective-permute-done | bytes 786464 | tf_op jit(solution)/shard_map/ppermute | solution.py:28
  32.9 3.1 pad_maximum_fusion.3
  37.2 4.5 collective-permute-start.2
  54.9 2.3 all-gather.2.cloned.1.call-done
  57.2 3.3 fusion.17
  63.6 3.8 pad_maximum_fusion
  67.3 2.2 slice_bitcast_fusion.12
  69.5 1.9 pad_maximum_fusion.2
  71.4 7.2 %reshape.242 = bf16[3456,4,128]{2,1,0:T(4,128)(2,1)} reshape(bf16[1,9,384,512]{3,2,1,0:T(8,128)(2,1)} %pad_maximum_fusion.2) | data formatting | bytes 7077888 | tf_op jit(solution)/shard_map/reshape.31
  78.7 6.8 %copy.102 = bf16[3456,4,128]{0,2,1:T(8,128)(2,1)} copy(bf16[3456,4,128]{2,1,0:T(4,128)(2,1)} %reshape.242) | data formatting | bytes 7077888 | tf_op jit(solution)/shard_map/reshape.31
  85.5 7.5 %bitcast_reduce_fusion = (f32[4,384]{1,0:T(4,128)S(1)}, f32[4,3456,384]{2,1,0:T(8,128)S(1)}) fusion(pred[3456]{0:T(1024)(128)(4,1)S(1)} %broadcast_in_dim.69, bf16[3456,4,128]{0,2,1:T(8,128)(2,1)} %copy.102, bf16[384,4,128]{2,1,0:T(4,128)(2,1)S(1)} %copy-done.10), kind=kOutput, calls=%fused_computation.2 | convolution fusion | flops 1374878208 | bytes 25175424 | tf_op jit(solution)/shard_map/while/body/eval_jaxpr/jqhd,jkhd->jhqk/dot_general | solution.py:34
  93.0 5.7 %fusion.1 = f32[4,384]{1,0:T(4,128)S(1)} fusion(f32[4,3456,384]{2,1,0:T(8,128)S(1)} %get-tuple-element.125, f32[4,384]{1,0:T(4,128)S(1)} %get-tuple-element.124, pred[3456]{0:T(1024)(128)(4,1)S(1)} %broadcast_in_dim.69), kind=kLoop, calls=%fused_computation.4 | loop fusion | flops 21232128 | bytes 21249408 | tf_op jit(solution)/shard_map/while/body/eval_jaxpr/reduce_sum | solution.py:92
  98.7 7.4 %fusion.3 = bf16[4,384,3456]{1,2,0:T(8,128)(2,1)} fusion(f32[4,3456,384]{2,1,0:T(8,128)S(1)} %get-tuple-element.125, f32[4,384]{1,0:T(4,128)S(1)} %log_add_fusion, pred[3456]{0:T(1024)(128)(4,1)S(1)} %broadcast_in_dim.69), kind=kLoop, calls=%fused_computation.6 | loop fusion | flops 21233664 | bytes 31860096 | tf_op jit(solution)/shard_map/while/body/eval_jaxpr/convert_element_type | solution.py:93
  106.1 2.0 pad_maximum_fusion.1
  108.0 7.5 %reshape.241 = bf16[3456,4,128]{2,1,0:T(4,128)(2,1)} reshape(bf16[1,9,384,512]{3,2,1,0:T(8,128)(2,1)} %pad_maximum_fusion.1) | data formatting | bytes 7077888 | tf_op jit(solution)/shard_map/reshape.41
  115.5 10.3 %convolution_bitcast_fusion = f32[1,3456,4,128]{1,3,2,0:T(8,128)} fusion(bf16[384,4,128]{0,2,1:T(8,128)(2,1)S(1)} %bitcast.185, bf16[4,384,3456]{1,2,0:T(8,128)(2,1)} %fusion.3), kind=kOutput, calls=%fused_computation.15 | convolution fusion | flops 1358954496 | bytes 18087936 | tf_op jit(solution)/shard_map/while/body/eval_jaxpr/jhqk,jqhd->jkhd/dot_general | solution.py:34
  125.8 6.3 %multiply_reduce_fusion = (f32[384,4]{0,1:T(4,128)S(1)}, bf16[4,128,384]{2,1,0:T(8,128)(2,1)S(1)}) fusion(f32[1,384,4,128]{1,3,2,0:T(8,128)S(1)} %bitcast.195, bf16[4,384,3456]{1,2,0:T(8,128)(2,1)} %fusion.3, bf16[3456,4,128]{2,1,0:T(4,128)(2,1)S(1)} %copy-done.3), kind=kOutput, calls=%fused_computation.75 | convolution fusion | flops 1359739392 | bytes 15341568 | tf_op jit(solution)/shard_map/while/body/eval_jaxpr/jhqk,jkhd->jqhd/dot_general | solution.py:34
  132.1 12.1 %multiply_convert_fusion = bf16[4,384,3456]{1,2,0:T(8,128)(2,1)} fusion(bf16[4,384,3456]{1,2,0:T(8,128)(2,1)} %fusion.3, bf16[384,4,128]{0,2,1:T(8,128)(2,1)S(1)} %bitcast.186, f32[4,384]{1,0:T(4,128)S(1)} %bitcast.197, bf16[3456,4,128]{2,1,0:T(4,128)(2,1)} %reshape.241), kind=kOutput, calls=%fused_computation.7 | convolution fusion | flops 1380188160 | bytes 25171968 | tf_op jit(solution)/shard_map/while/body/eval_jaxpr/jqhd,jkhd->jhqk/dot_general | solution.py:34
  144.2 9.1 %copy.108 = f32[1,3456,4,128]{3,2,0,1:T(4,128)} copy(f32[1,3456,4,128]{1,3,2,0:T(8,128)} %convolution_bitcast_fusion) | data formatting | bytes 14155776 | tf_op jit(solution)/shard_map/while/body/eval_jaxpr/jhqk,jqhd->jkhd/transpose | solution.py:34
  153.3 8.3 %slice_bitcast_fusion.23 = (f32[1,384,512]{2,0,1:T(1,128)}, f32[1,384,512]{2,0,1:T(1,128)}, f32[1,384,512]{2,0,1:T(1,128)}, f32[1,384,512]{2,0,1:T(1,128)}, f32[...) fusion(f32[1,3,3,384,512]{4,0,3,2,1:T(1,128)} %bitcast.183), kind=kLoop, calls=%fused_computation.64 | loop fusion | bytes 14155776 | tf_op jit(solution)/shard_map/while/body/eval_jaxpr/squeeze | solution.py:64
  161.7 2.9 multiply_bitcast_fusion
  164.6 25.5 %copy.105 = f32[1,3456,4,128]{3,2,0,1:T(4,128)S(1)} copy(f32[1,3456,4,128]{3,1,2,0:T(8,128)S(1)} %multiply_bitcast_fusion) | data formatting | bytes 14155776 | tf_op jit(solution)/shard_map/while/body/eval_jaxpr/mul | solution.py:120
  190.2 4.2 slice_bitcast_fusion.32
  194.3 4.4 fusion.9
  200.4 3.1 add_bitcast_fusion
  203.5 3.3 add_bitcast_fusion.1
  206.8 3.2 add_bitcast_fusion.2
  210.0 10.9 %maximum_bitcast_fusion.2 = f32[1,3,3,384,512]{4,2,3,1,0:T(4,128)} fusion(f32[1,3,384,512]{3,1,2,0:T(4,128)} %add_bitcast_fusion, f32[1,3,384,512]{3,1,2,0:T(4,128)} %add_bitcast_fusion.1, f32[1,3,384,512]{3,1,2,0:T(4,128)} %add_bitcast_fusion.2), kind=kLoop, calls=%fused_computation.12 | loop fusion | flops 3538944 | bytes 14155776 | tf_op jit(solution)/shard_map/while/body/eval_jaxpr/stack | solution.py:198
  220.9 3.2 add_bitcast_fusion.3
  224.1 3.2 add_bitcast_fusion.4
  227.2 3.1 add_bitcast_fusion.5
  230.4 10.1 %maximum_bitcast_fusion.1 = f32[1,3,3,384,512]{4,2,3,1,0:T(4,128)} fusion(f32[1,3,384,512]{3,1,2,0:T(4,128)} %add_bitcast_fusion.3, f32[1,3,384,512]{3,1,2,0:T(4,128)} %add_bitcast_fusion.4, f32[1,3,384,512]{3,1,2,0:T(4,128)} %add_bitcast_fusion.5), kind=kLoop, calls=%fused_computation.11 | loop fusion | flops 3538944 | bytes 14155776 | tf_op jit(solution)/shard_map/while/body/eval_jaxpr/stack | solution.py:198
  240.5 10.7 %maximum_bitcast_fusion = f32[1,1,2,3,3,384,512]{6,4,5,3,2,1,0:T(4,128)S(1)} fusion(f32[1,3,3,384,512]{4,2,3,1,0:T(4,128)} %maximum_bitcast_fusion.2, f32[1,3,3,384,512]{4,2,3,1,0:T(4,128)} %maximum_bitcast_fusion.1), kind=kLoop, calls=%fused_computation.9 | loop fusion | flops 3538944 | bytes 28311552 | tf_op jit(solution)/shard_map/reshape | solution.py:203
  251.2 7.8 %slice_bitcast_fusion.2 = (f32[1,1,2,3,384,512]{5,3,4,2,1,0:T(4,128)}, f32[1,1,2,3,384,512]{5,3,4,2,1,0:T(4,128)}, f32[1,1,2,3,384,512]{5,3,4,2,1,0:T(4,128)}) fusion(f32[1,1,2,3,3,384,512]{6,4,5,3,2,1,0:T(4,128)S(1)} %maximum_bitcast_fusion), kind=kLoop, calls=%fused_computation.20 | loop fusion | bytes 28311552 | tf_op jit(solution)/shard_map/squeeze | solution.py:209
  259.0 18.3 %pad_add_fusion = (f32[1,3,2,3,384,512]{5,3,4,2,1,0:T(4,128)}, bf16[1,3,2,3,384,512]{5,3,4,2,1,0:T(4,128)(2,1)S(1)}) fusion(f32[1,1,2,3,384,512]{5,3,4,2,1,0:T(4,128)} %get-tuple-element.86, f32[1,1,2,3,384,512]{5,3,4,2,1,0:T(4,128)} %get-tuple-element.87, f32[1,1,2,3,384,512]{5,3,4,2,1,0:T(4,128)} %get-tuple-element.85), kind=kLoop, calls=%fused_computation.10 | loop fusion | flops 10616832 | bytes 35389440 | tf_op jit(solution)/shard_map/add | solution.py:212
  277.3 2.2 slice_bitcast_fusion.4
  279.5 2.0 copy.113
  281.5 3.5 collective-permute-start.5
  285.0 2.0 copy.111
  288.3 71.1 %all-reduce.24.cloned.1.call-done = f32[512,3072]{1,0:T(8,128)} async-done(((f32[512,3072]{1,0:T(8,128)}), f32[512,3072]{1,0:T(8,128)}) %all-reduce.24.cloned.1.call-update) | async-done | bytes 6291472 | tf_op jit(solution)/shard_map/psum | solution.py:238
  359.4 12.9 %fusion.24 = (bf16[1,1,2,3,384,512]{5,3,4,2,1,0:T(4,128)(2,1)S(1)}, f32[1,1,2,3,384,512]{5,3,4,2,1,0:T(4,128)}) fusion(bf16[1,2,3,384,512]{4,3,2,1,0:T(8,128)(2,1)S(1)} %collective-permute-done.5, bf16[1,2,3,384,512]{4,3,2,1,0:T(8,128)(2,1)} %collective-permute-done.4, f32[1,3,2,3,384,512]{5,3,4,2,1,0:T(4,128)} %get-tuple-element.83), kind=kLoop, calls=%fused_computation.84 | loop fusion | flops 5898240 | bytes 16515072 | tf_op jit(solution)/shard_map/convert.6
  372.3 3.4 slice_bitcast_fusion.6
  378.9 6.3 %convolution_multiply_fusion = f32[4,128,384]{2,1,0:T(8,128)S(1)} fusion(bf16[3456,4,128]{0,2,1:T(8,128)(2,1)S(1)} %copy-done.4, bf16[4,384,3456]{1,2,0:T(8,128)(2,1)} %multiply_convert_fusion), kind=kOutput, calls=%fused_computation.45 | convolution fusion | flops 1359151104 | bytes 14942208 | tf_op jit(solution)/shard_map/while/body/eval_jaxpr/jhqk,jkhd->jqhd/dot_general | solution.py:34
  386.4 4.8 fusion.5
  392.4 7.1 %fusion.13 = f32[1,1,2,1,384,512]{5,3,4,2,1,0:T(1,128)S(1)} fusion(f32[1,1,2,3,384,512]{5,3,4,2,1,0:T(4,128)} %get-tuple-element.82, bf16[1,1,2,384,512]{4,0,3,2,1:T(2,128)(2,1)} %copy-done.33, bf16[1,1,2,384,512]{4,0,3,2,1:T(2,128)(2,1)} %collective-permute-done.6), kind=kLoop, calls=%fused_computation.44 | loop fusion | flops 1572864 | bytes 4718592 | tf_op jit(solution)/shard_map/add | solution.py:225
  402.4 99.8 %all-reduce.26.cloned.1.call-done = f32[512,3072]{1,0:T(8,128)} async-done(((f32[512,3072]{1,0:T(8,128)}), f32[512,3072]{1,0:T(8,128)}) %all-reduce.26.cloned.1.call-update) | async-done | bytes 6291472 | tf_op jit(solution)/shard_map/psum | solution.py:238
  502.2 3.9 constant_dynamic-slice_fusion
  (103 shorter events, 22.0 us)
Async XLA Ops:
  7.2 50.0 %copy-start = (bf16[1,1,1,384,3072]{4,3,2,1,0:T(8,128)(2,1)S(1)}, bf16[1,1,1,384,3072]{4,3,2,1,0:T(8,128)(2,1)}, u32[]{:S(2)}) copy-start(bf16[1,1,1,384,3072]{4,3,2,1,0:T(8,128)(2,1)} %param.8) | copy-start | bytes 7077892
  7.2 50.0 %all-gather.2.cloned.1.call-start = ((), (), s32[]{:S(2)}) async-start(), calls=%async_computation | async-start | bytes 4718592 | tf_op jit(solution)/shard_map/all_gather | solution.py:154
  7.9 46.1 %copy-start.34 = (bf16[1,1,1,384,512]{4,3,2,1,0:T(8,128)(2,1)S(1)}, bf16[1,1,1,384,512]{4,3,2,1,0:T(8,128)(2,1)}, u32[]{:S(2)}) copy-start(bf16[1,1,1,384,512]{4,3,2,1,0:T(8,128)(2,1)} %param.5) | copy-start | bytes 1179652
  7.9 351.4 %all-reduce.24.cloned.1.call-start = ((), (), s32[]{:S(2)}) async-start(), calls=%async_computation.1 | async-start | bytes 12582912 | tf_op jit(solution)/shard_map/psum | solution.py:238
  9.2 22.5 %collective-permute-start.1 = (bf16[2,1,1,1,384,512]{5,4,3,2,1,0:T(8,128)(2,1)S(1)}, bf16[2,1,1,1,384,512]{5,4,3,2,1,0:T(8,128)(2,1)S(1)}, u32[]{:S(2)}, u32[]{:S(2)}) collective-permute-start(bf16[2,1,1,1,384,512]{5,4,3,2,1,0:T(8,128)(2,1)S(1)} %pad_maximum_fusion.4), channel_id=1, source_target_pairs={{4,0},{8,4},{12,8},{5,1},{9,5},{13,9},{6,2},{10,6},{14,10},{7,3},{... | collective-permute-start | bytes 2359304 | tf_op jit(solution)/shard_map/ppermute | solution.py:28
  10.5 22.4 %collective-permute-start = (bf16[2,1,1,1,384,512]{5,4,3,2,1,0:T(8,128)(2,1)S(1)}, bf16[2,1,1,1,384,512]{5,4,3,2,1,0:T(8,128)(2,1)S(1)}, u32[]{:S(2)}, u32[]{:S(2)}) collective-permute-start(bf16[2,1,1,1,384,512]{5,4,3,2,1,0:T(8,128)(2,1)S(1)} %pad_maximum_fusion.4), channel_id=1, source_target_pairs={{0,4},{4,8},{8,12},{1,5},{5,9},{9,13},{2,6},{6,10},{10,14},{3,7},{... | collective-permute-start | bytes 2359304 | tf_op jit(solution)/shard_map/ppermute | solution.py:27
  31.7 1.2 copy-start.12
  32.9 3.1 copy-start.13
  36.0 27.6 %collective-permute-start.3 = (bf16[2,1,3,1,384,512]{5,4,3,2,1,0:T(8,128)(2,1)}, bf16[2,1,3,1,384,512]{5,4,3,2,1,0:T(8,128)(2,1)}, u32[]{:S(2)}, u32[]{:S(2)}) collective-permute-start(bf16[2,1,3,1,384,512]{5,4,3,2,1,0:T(8,128)(2,1)} %pad_maximum_fusion.3), channel_id=1, source_target_pairs={{1,0},{2,1},{3,2},{5,4},{6,5},{7,6},{9,8},{10,9},{11,10},{13,12},{... | collective-permute-start | bytes 7077896 | tf_op jit(solution)/shard_map/ppermute | solution.py:28
  37.2 26.3 %collective-permute-start.2 = (bf16[2,1,3,1,384,512]{5,4,3,2,1,0:T(8,128)(2,1)}, bf16[2,1,3,1,384,512]{5,4,3,2,1,0:T(8,128)(2,1)}, u32[]{:S(2)}, u32[]{:S(2)}) collective-permute-start(bf16[2,1,3,1,384,512]{5,4,3,2,1,0:T(8,128)(2,1)} %pad_maximum_fusion.3), channel_id=1, source_target_pairs={{0,1},{1,2},{2,3},{4,5},{5,6},{6,7},{8,9},{9,10},{10,11},{12,13},{... | collective-permute-start | bytes 7077896 | tf_op jit(solution)/shard_map/ppermute | solution.py:27
  54.9 8.7 %copy-start.8 = (bf16[1,1,1,384,512]{4,3,2,1,0:T(8,128)(2,1)S(1)}, bf16[1,1,1,384,512]{4,3,2,1,0:T(8,128)(2,1)}, u32[]{:S(2)}) copy-start(bf16[1,1,1,384,512]{4,3,2,1,0:T(8,128)(2,1)} %param.7) | copy-start | bytes 1179652
  54.9 8.7 %copy-start.9 = (bf16[1,1,1,384,512]{4,3,2,1,0:T(8,128)(2,1)S(1)}, bf16[1,1,1,384,512]{4,3,2,1,0:T(8,128)(2,1)}, u32[]{:S(2)}) copy-start(bf16[1,1,1,384,512]{4,3,2,1,0:T(8,128)(2,1)} %param.6) | copy-start | bytes 1179652
  60.5 0.7 copy-start.32
  78.7 6.8 %copy-start.10 = (bf16[384,4,128]{2,1,0:T(4,128)(2,1)S(1)}, bf16[384,4,128]{2,1,0:T(4,128)(2,1)}, u32[]{:S(2)}) copy-start(bf16[384,4,128]{2,1,0:T(4,128)(2,1)} %reshape.243) | copy-start | bytes 1179652
  98.7 7.4 %copy-start.5 = (bf16[1,3,384,512]{3,2,1,0:T(8,128)(2,1)S(1)}, bf16[1,3,384,512]{3,2,1,0:T(8,128)(2,1)}, u32[]{:S(2)}) copy-start(bf16[1,3,384,512]{3,2,1,0:T(8,128)(2,1)} %get-tuple-element.108) | copy-start | bytes 3538948
  98.7 7.4 %copy-start.6 = (bf16[1,3,384,512]{3,2,1,0:T(8,128)(2,1)S(1)}, bf16[1,3,384,512]{3,2,1,0:T(8,128)(2,1)}, u32[]{:S(2)}) copy-start(bf16[1,3,384,512]{3,2,1,0:T(8,128)(2,1)} %get-tuple-element.112) | copy-start | bytes 3538948
  98.7 7.4 %copy-start.7 = (bf16[1,3,384,512]{3,2,1,0:T(8,128)(2,1)S(1)}, bf16[1,3,384,512]{3,2,1,0:T(8,128)(2,1)}, u32[]{:S(2)}) copy-start(bf16[1,3,384,512]{3,2,1,0:T(8,128)(2,1)} %get-tuple-element.113) | copy-start | bytes 3538948
  115.5 10.3 %copy-start.3 = (bf16[3456,4,128]{2,1,0:T(4,128)(2,1)S(1)}, bf16[3456,4,128]{2,1,0:T(4,128)(2,1)}, u32[]{:S(2)}) copy-start(bf16[3456,4,128]{2,1,0:T(4,128)(2,1)} %reshape.241) | copy-start | bytes 10616836
  115.5 10.3 %copy-start.11 = (f32[384,512]{0,1:T(8,128)S(1)}, f32[384,512]{0,1:T(8,128)}, u32[]{:S(2)}) copy-start(f32[384,512]{0,1:T(8,128)} %copy.100) | copy-start | bytes 2359300
  153.3 8.3 %copy-start.2 = (bf16[4,384,3456]{1,2,0:T(8,128)(2,1)S(1)}, bf16[4,384,3456]{1,2,0:T(8,128)(2,1)}, u32[]{:S(2)}) copy-start(bf16[4,384,3456]{1,2,0:T(8,128)(2,1)} %multiply_convert_fusion) | copy-start | bytes 31850500
  198.8 1.1 copy-start.29
  198.8 1.4 copy-start.30
  198.8 1.6 copy-start.31
  198.8 303.5 %all-reduce.26.cloned.1.call-start = ((), (), s32[]{:S(2)}) async-start(), calls=%async_computation.2 | async-start | bytes 12582912 | tf_op jit(solution)/shard_map/psum | solution.py:238
  198.8 4.7 copy-start.26
  198.9 4.7 copy-start.27
  198.9 4.7 copy-start.28
  203.5 3.3 copy-start.20
  203.5 3.3 copy-start.21
  203.5 3.3 copy-start.22
  210.0 10.9 %copy-start.23 = (f32[1,384,512]{2,0,1:T(1,128)S(1)}, f32[1,384,512]{2,0,1:T(1,128)}, u32[]{:S(2)}) copy-start(f32[1,384,512]{2,0,1:T(1,128)} %get-tuple-element.91) | copy-start | bytes 2359300
  210.0 10.9 %copy-start.24 = (f32[1,384,512]{2,0,1:T(1,128)S(1)}, f32[1,384,512]{2,0,1:T(1,128)}, u32[]{:S(2)}) copy-start(f32[1,384,512]{2,0,1:T(1,128)} %get-tuple-element.92) | copy-start | bytes 2359300
  210.0 10.9 %copy-start.25 = (f32[1,384,512]{2,0,1:T(1,128)S(1)}, f32[1,384,512]{2,0,1:T(1,128)}, u32[]{:S(2)}) copy-start(f32[1,384,512]{2,0,1:T(1,128)} %get-tuple-element.93) | copy-start | bytes 2359300
  220.9 3.2 copy-start.17
  220.9 3.2 copy-start.18
  220.9 3.2 copy-start.19
  224.1 3.2 copy-start.14
  224.1 3.2 copy-start.15
  224.1 3.2 copy-start.16
  281.5 77.9 %collective-permute-start.5 = (bf16[1,2,3,384,512]{4,3,2,1,0:T(8,128)(2,1)}, bf16[1,2,3,384,512]{4,3,2,1,0:T(8,128)(2,1)S(1)}, u32[]{:S(2)}, u32[]{:S(2)}) collective-permute-start(bf16[1,2,3,384,512]{4,3,2,1,0:T(8,128)(2,1)} %copy.113), channel_id=1, source_target_pairs={{0,4},{4,8},{8,12},{1,5},{5,9},{9,13},{2,6},{6,10},{10,14},{3,7},{... | collective-permute-start | bytes 7077896 | tf_op jit(solution)/shard_map/ppermute | solution.py:17
  287.0 72.4 %collective-permute-start.4 = (bf16[1,2,3,384,512]{4,3,2,1,0:T(8,128)(2,1)}, bf16[1,2,3,384,512]{4,3,2,1,0:T(8,128)(2,1)}, u32[]{:S(2)}, u32[]{:S(2)}) collective-permute-start(bf16[1,2,3,384,512]{4,3,2,1,0:T(8,128)(2,1)} %copy.111), channel_id=1, source_target_pairs={{4,0},{8,4},{12,8},{5,1},{9,5},{13,9},{6,2},{10,6},{14,10},{7,3},{... | collective-permute-start | bytes 7077896 | tf_op jit(solution)/shard_map/ppermute | solution.py:17
  372.3 6.6 %copy-start.4 = (bf16[3456,4,128]{0,2,1:T(8,128)(2,1)S(1)}, bf16[3456,4,128]{0,2,1:T(8,128)(2,1)}, u32[]{:S(2)}) copy-start(bf16[3456,4,128]{0,2,1:T(8,128)(2,1)} %copy.102) | copy-start | bytes 10616836
  375.7 15.5 %collective-permute-start.7 = (bf16[1,1,2,384,512]{4,0,3,2,1:T(2,128)(2,1)}, bf16[1,1,2,384,512]{4,0,3,2,1:T(2,128)(2,1)S(1)}, u32[]{:S(2)}, u32[]{:S(2)}) collective-permute-start(bf16[1,1,2,384,512]{4,0,3,2,1:T(2,128)(2,1)} %get-tuple-element.115), channel_id=1, source_target_pairs={{0,1},{1,2},{2,3},{4,5},{5,6},{6,7},{8,9},{9,10},{10,11},{12,13},{... | collective-permute-start | bytes 2359304 | tf_op jit(solution)/shard_map/ppermute | solution.py:17
  377.4 13.8 %collective-permute-start.6 = (bf16[1,1,2,384,512]{4,0,3,2,1:T(2,128)(2,1)}, bf16[1,1,2,384,512]{4,0,3,2,1:T(2,128)(2,1)}, u32[]{:S(2)}, u32[]{:S(2)}) collective-permute-start(bf16[1,1,2,384,512]{4,0,3,2,1:T(2,128)(2,1)} %get-tuple-element.114), channel_id=1, source_target_pairs={{1,0},{2,1},{3,2},{5,4},{6,5},{7,6},{9,8},{10,9},{11,10},{13,12},{... | collective-permute-start | bytes 2359304 | tf_op jit(solution)/shard_map/ppermute | solution.py:17
  391.2 1.2 copy-start.33
  401.5 104.7 %copy-start.1 = (bf16[1,1,1,384,3072]{4,3,2,1,0:T(8,128)(2,1)S(1)}, bf16[1,1,1,384,3072]{4,3,2,1,0:T(8,128)(2,1)}, u32[]{:S(2)}) copy-start(bf16[1,1,1,384,3072]{4,3,2,1,0:T(8,128)(2,1)} %param.8) | copy-start | bytes 7077892
Sparse Core Ops, SparseCore 0:
  9.5 47.6 all-gather.1
  198.9 160.3 all-reduce.23
  363.0 139.2 all-reduce.25
